TPU v7x, 256 devices: a whole 4x4x8 slice. The times are simulated.
256 devices in a mesh: gx: 32 (over y, z), gy: 8 (over x, core).
Axes of the slice: x: 4, y: 4, z: 8, core: 2. Of those that a mesh axis runs over, the one named last changes fastest.
Arguments:
- features: bfloat16 [2048, 64, 512], P(('gx', 'gy')), may hold values from -6 to 6
- neighbours: int32 [2048, 6], P(('gx', 'gy')), may hold values from 0 to 16, as said below
- counts: int32 [256], P(('gx', 'gy')), may hold values from 1 to 8, as said below
- conv_weight: bfloat16 [64, 448], replicated, may hold values from -0.25 to 0.25
- down_weight: bfloat16 [128, 512], replicated, may hold values from -0.25 to 0.25
- head_weight: bfloat16 [128, 128], replicated, may hold values from -0.5 to 0.5
- coarse_map: int32 [256, 8], P(('gx', 'gy')), may hold values from 0 to 32, as said below
- latent_grad: bfloat16 [256, 512, 128], P(('gx', 'gy')), may hold values from -6 to 6
Outputs:
- latent: bfloat16 [256, 512, 128], P(('gx', 'gy'))
- features_grad: bfloat16 [2048, 64, 512], P(('gx', 'gy'))
- conv_grad: float32 [64, 448], replicated
- down_grad: float32 [128, 512], replicated
- head_grad: float32 [128, 128], replicated
Inputs may be any that keep to these rules, and one draw needn't show every extreme that they name: `counts`: in every draw, max(1, (devices along gx times devices along gy) // 8) columns have exactly 8 active blocks; each other column has between 1 and 4. 16 means no neighbour; a value below 8 is an active slot of the same column; a value v of 8 or more is the active slot v - 8 of the adjacent column in that direction; the z directions never name another column; inactive slots have no neighbours. `coarse_map`: 32 marks an empty octant; every other entry names an active block's octant, and each such octant is named at most once among the four columns that share a merged list.
All inputs are finite; a program needn't handle non-finite values.
Results may differ from a plain program's by a relative error of at most 0.013.
Values may be sent and summed in bfloat16 or wider, within the bound.
A program may use at most 128 MiB of HBM per device.

v0:
```python
import jax
import jax.numpy as jnp
from jax import lax
from jax.sharding import PartitionSpec as P


def from_partner(block, axis, distance):
    count = lax.axis_size(axis)
    route = []
    for low in range(count):
        high = low | 1 << distance
        if high != low and high < count:
            route += [(low, high), (high, low)]
    return lax.ppermute(block, axis, route)


def padded(block, sides, width):
    for axis, dim in sides:
        count = lax.axis_size(axis)
        forward = [(i, i + 1) for i in range(count - 1)]
        backward = [(target, source) for source, target in forward]
        low = lax.ppermute(
            lax.slice_in_dim(block, block.shape[dim] - width, None, axis=dim), axis, forward
        )
        high = lax.ppermute(lax.slice_in_dim(block, 0, width, axis=dim), axis, backward)
        block = jnp.concatenate([low, block, high], axis=dim)
    return block


def silu_grad(values):
    sigmoid_value = jax.nn.sigmoid(values)
    return sigmoid_value * (1.0 + values * (1.0 - sigmoid_value))


def octet(volume):
    return volume.reshape(volume.shape[0], volume.shape[1], 2, 2, 2, 4, 4, 4)


def face_of(cube, axis_number, upper):
    number, channels = (cube.shape[0], cube.shape[1])
    plane = lax.index_in_dim(cube, 3 if upper else 0, 5 + axis_number, keepdims=False)
    plane = lax.index_in_dim(plane, 1 if upper else 0, 2 + axis_number, keepdims=False)
    return plane.reshape(number, channels * 64)


def face_index(axis_number, upper):
    index = [slice(None)] * 8
    index[2 + axis_number] = 1 if upper else 0
    index[5 + axis_number] = 3 if upper else 0
    return tuple(index)


def expand_plane(rows, cube, axis_number):
    number, channels = (cube.shape[0], cube.shape[1])
    return jnp.expand_dims(
        rows.reshape(number, channels, 2, 2, 4, 4), (2 + axis_number, 5 + axis_number)
    )


def shift_minus(cube, rows, axis_number):
    parity, place = (2 + axis_number, 5 + axis_number)
    plane = expand_plane(rows, cube, axis_number)
    lower = lax.slice_in_dim(cube, 0, 1, axis=parity)
    upper = lax.slice_in_dim(cube, 1, 2, axis=parity)
    out_low = jnp.concatenate([plane, lax.slice_in_dim(upper, 0, 3, axis=place)], axis=place)
    return jnp.concatenate([out_low, lower], axis=parity)


def shift_plus(cube, rows, axis_number):
    parity, place = (2 + axis_number, 5 + axis_number)
    plane = expand_plane(rows, cube, axis_number)
    lower = lax.slice_in_dim(cube, 0, 1, axis=parity)
    upper = lax.slice_in_dim(cube, 1, 2, axis=parity)
    out_high = jnp.concatenate([lax.slice_in_dim(lower, 1, 4, axis=place), plane], axis=place)
    return jnp.concatenate([upper, out_high], axis=parity)


def minus_back(grad_out, axis_number):
    parity, place = (2 + axis_number, 5 + axis_number)
    grad_low = lax.slice_in_dim(grad_out, 0, 1, axis=parity)
    grad_high = lax.slice_in_dim(grad_out, 1, 2, axis=parity)
    moved = jnp.concatenate(
        [
            lax.slice_in_dim(grad_low, 1, 4, axis=place),
            jnp.zeros_like(lax.slice_in_dim(grad_low, 0, 1, axis=place)),
        ],
        axis=place,
    )
    plane = lax.index_in_dim(
        lax.index_in_dim(grad_low, 0, place, keepdims=False), 0, parity, keepdims=False
    )
    return (jnp.concatenate([grad_high, moved], axis=parity), plane)


def plus_back(grad_out, axis_number):
    parity, place = (2 + axis_number, 5 + axis_number)
    grad_low = lax.slice_in_dim(grad_out, 0, 1, axis=parity)
    grad_high = lax.slice_in_dim(grad_out, 1, 2, axis=parity)
    moved = jnp.concatenate(
        [
            jnp.zeros_like(lax.slice_in_dim(grad_high, 0, 1, axis=place)),
            lax.slice_in_dim(grad_high, 0, 3, axis=place),
        ],
        axis=place,
    )
    plane = lax.index_in_dim(
        lax.index_in_dim(grad_high, 3, place, keepdims=False), 0, parity, keepdims=False
    )
    return (jnp.concatenate([moved, grad_low], axis=parity), plane)


def face_layers(cube):
    return (
        face_of(cube, 0, True),
        face_of(cube, 0, False),
        face_of(cube, 1, True),
        face_of(cube, 1, False),
        face_of(cube, 2, True),
        face_of(cube, 2, False),
    )


def pick_rows(local_rows, remote_rows, index):
    width = local_rows.shape[1]
    pooled = jnp.concatenate(
        [local_rows, remote_rows, jnp.zeros((1, width), local_rows.dtype)], axis=0
    )
    return pooled[index]


def neighbour_stack(cube, faces, remotes, links):
    number, channels = (cube.shape[0], cube.shape[1])
    blank = jnp.zeros_like(faces[4])
    sources = (remotes[0], remotes[1], remotes[2], remotes[3], blank, blank)
    picked = [
        pick_rows(faces[direction], sources[direction], links[:, direction])
        for direction in range(6)
    ]
    fields = [
        cube,
        shift_minus(cube, picked[0], 0),
        shift_plus(cube, picked[1], 0),
        shift_minus(cube, picked[2], 1),
        shift_plus(cube, picked[3], 1),
        shift_minus(cube, picked[4], 2),
        shift_plus(cube, picked[5], 2),
    ]
    return jnp.stack(fields, axis=1).reshape(number, 7 * channels, 512)


def stack_grad(taps_grad, links):
    number, channels = (taps_grad.shape[0], taps_grad.shape[1] // 7)
    parts = taps_grad.reshape(number, 7, channels, 2, 2, 2, 4, 4, 4)
    grad_cube = parts[:, 0]
    face_grads = []
    for direction in range(6):
        axis_number = direction // 2
        if direction % 2 == 0:
            moved, plane = minus_back(parts[:, direction + 1], axis_number)
        else:
            moved, plane = plus_back(parts[:, direction + 1], axis_number)
        grad_cube = grad_cube + moved
        face_grads.append(plane.reshape(number, channels * 64))
    pools = [
        jnp.zeros((2 * number + 1, channels * 64), jnp.float32)
        .at[links[:, direction]]
        .add(face_grads[direction])
        for direction in range(6)
    ]
    for direction in range(6):
        shaped = pools[direction][:number].reshape(number, channels, 2, 2, 4, 4)
        grad_cube = grad_cube.at[face_index(direction // 2, direction % 2 == 0)].add(shaped)
    far_rows = [
        pools[direction][number : 2 * number].astype(jnp.bfloat16) for direction in range(4)
    ]
    return (grad_cube, far_rows)


def add_faces(grad_cube, into_xhigh, into_xlow, into_yhigh, into_ylow):
    number, channels = (grad_cube.shape[0], grad_cube.shape[1])

    def planes(rows):
        return rows.astype(jnp.float32).reshape(number, channels, 2, 2, 4, 4)

    grad_cube = grad_cube.at[face_index(0, True)].add(planes(into_xhigh))
    grad_cube = grad_cube.at[face_index(0, False)].add(planes(into_xlow))
    grad_cube = grad_cube.at[face_index(1, True)].add(planes(into_yhigh))
    grad_cube = grad_cube.at[face_index(1, False)].add(planes(into_ylow))
    return grad_cube


def merge_pool(own_rows):
    beside_y = from_partner(own_rows, "gy", 0)
    received = from_partner(jnp.concatenate([own_rows, beside_y], axis=0), "gx", 0)
    half = own_rows.shape[0]
    return jnp.concatenate([own_rows, received[:half], beside_y, received[half:]], axis=0)


def split_pool(back_rows):
    half = back_rows.shape[0] // 4
    own_part = back_rows[:half].astype(jnp.float32)
    along_x = back_rows[half : 2 * half]
    along_y = back_rows[2 * half : 3 * half]
    diagonal = back_rows[3 * half :]
    returned = from_partner(jnp.concatenate([along_x, diagonal], axis=0), "gx", 0)
    kept = own_part + returned[:half].astype(jnp.float32)
    beside = (along_y.astype(jnp.float32) + returned[half:].astype(jnp.float32)).astype(
        jnp.bfloat16
    )
    final_rows = kept + from_partner(beside, "gy", 0).astype(jnp.float32)
    return final_rows.astype(jnp.bfloat16)


def scatter_rows(volume, links, number):
    width = volume.shape[1] * volume.shape[2] // 8
    rows = volume.reshape(volume.shape[0] * 8, width)
    total = (
        jnp.zeros((4 * number + 1, width), jnp.float32)
        .at[links.reshape(-1)]
        .add(rows.astype(jnp.float32))
    )
    return total[: 4 * number].astype(jnp.bfloat16)


def body(
    features, neighbours, counts, conv_weight, down_weight, head_weight, coarse_map, latent_grad
):
    number, channels = (features.shape[0], features.shape[1])
    wide = down_weight.shape[0]
    coarse_count = coarse_map.shape[0]
    active = jnp.arange(number) < counts[0]
    masked = jnp.where(active[:, None, None], features, jnp.zeros((), jnp.bfloat16))
    cube = octet(masked)
    faces = face_layers(cube)
    rim_x = padded(jnp.stack([faces[1], faces[0]]), (("gx", 0),), 1)
    rim_y = padded(jnp.stack([faces[3], faces[2]]), (("gy", 0),), 1)
    taps = neighbour_stack(cube, faces, (rim_x[0], rim_x[3], rim_y[0], rim_y[3]), neighbours)
    hidden = jnp.einsum("ok,bkv->bov", conv_weight, taps, preferred_element_type=jnp.float32)
    act = jax.nn.silu(hidden).astype(jnp.bfloat16)
    patches = act.reshape(number, channels * 8, 64)
    octants = jnp.einsum(
        "ok,bkv->bvo", down_weight, patches, preferred_element_type=jnp.float32
    ).astype(jnp.bfloat16)
    empty_row = jnp.zeros((1, 64 * wide), jnp.bfloat16)
    merged = merge_pool(octants.reshape(number, 64 * wide))
    coarse = jnp.concatenate([merged, empty_row], axis=0)[coarse_map].reshape(
        coarse_count, 512, wide
    )
    coarse_act = jax.nn.silu(coarse.astype(jnp.float32)).astype(jnp.bfloat16)
    latent = jnp.einsum(
        "oi,cvi->cvo", head_weight, coarse_act, preferred_element_type=jnp.float32
    ).astype(jnp.bfloat16)
    act_grad = jnp.einsum(
        "oi,cvo->cvi", head_weight, latent_grad, preferred_element_type=jnp.float32
    )
    coarse_grad = (act_grad * silu_grad(coarse.astype(jnp.float32))).astype(jnp.bfloat16)
    head_part = jnp.einsum(
        "cvo,cvi->oi", latent_grad, coarse_act, preferred_element_type=jnp.float32
    )
    octant_grad = split_pool(scatter_rows(coarse_grad, coarse_map, number)).reshape(
        number, 64, wide
    )
    down_part = jnp.einsum("bvo,bkv->ok", octant_grad, patches, preferred_element_type=jnp.float32)
    patch_grad = jnp.einsum(
        "ok,bvo->bkv", down_weight, octant_grad, preferred_element_type=jnp.float32
    )
    hidden_grad = (patch_grad.reshape(number, channels, 512) * silu_grad(hidden)).astype(
        jnp.bfloat16
    )
    conv_part = jnp.einsum("bov,bkv->ok", hidden_grad, taps, preferred_element_type=jnp.float32)
    taps_grad = jnp.einsum(
        "ok,bov->bkv", conv_weight, hidden_grad, preferred_element_type=jnp.float32
    )
    near_grad, far_rows = stack_grad(taps_grad, neighbours)
    return_x = padded(jnp.stack([far_rows[0], far_rows[1]]), (("gx", 0),), 1)
    return_y = padded(jnp.stack([far_rows[2], far_rows[3]]), (("gy", 0),), 1)
    total_grad = add_faces(near_grad, return_x[3], return_x[0], return_y[3], return_y[0]).reshape(
        number, channels, 512
    )
    features_grad = jnp.where(active[:, None, None], total_grad, 0.0).astype(jnp.bfloat16)
    summed = lax.psum((conv_part, down_part, head_part), ("gx", "gy"))
    scale = float(number * lax.axis_size("gx") * lax.axis_size("gy")) ** (-0.5)
    return (latent, features_grad, summed[0] * scale, summed[1] * scale, summed[2] * scale)


def solution(mesh):
    placed = (
        P(("gx", "gy"), None, None),
        P(("gx", "gy"), None),
        P(("gx", "gy")),
        P(),
        P(),
        P(),
        P(("gx", "gy"), None),
        P(("gx", "gy"), None, None),
    )
    return jax.shard_map(
        body,
        mesh=mesh,
        in_specs=placed,
        out_specs=(P(("gx", "gy"), None, None), P(("gx", "gy"), None, None), P(), P(), P()),
        check_vma=False,
    )
```

profile of v0, /device:TPU:2, one launch (start us, length us, event | category | flops | bytes accessed | tf_op | source)
XLA Modules:
  0.0 611.6 jit_solution(5561831385059505792)
XLA Ops:
  12.5 4.4 collective-permute-start
  21.6 3.1 copy.127
  34.7 3.8 collective-permute-start.3
  90.8 11.2 %copy.151 = bf16[8,7,64,2,2,2,4,4,4]{2,1,8,7,6,5,4,3,0:T(8,128)(2,1)} copy(bf16[8,7,64,2,2,2,4,4,4]{2,0,8,7,6,5,4,3,1:T(8,128)(2,1)} %fusion.16) | data formatting | bytes 7340032 | tf_op jit(solution)/shard_map/stack | solution.py:148
  102.0 11.6 %reshape.747 = bf16[8,448,512]{1,2,0:T(8,128)(2,1)} reshape(bf16[8,7,64,2,2,2,4,4,4]{2,1,8,7,6,5,4,3,0:T(8,128)(2,1)} %copy.151) | data formatting | bytes 7340032 | tf_op jit(solution)/shard_map/reshape | solution.py:148
  113.6 4.6 multiply_convert_fusion.1
  123.7 6.5 %collective-permute-done.5 = bf16[16,8192]{1,0:T(8,128)(2,1)S(1)} collective-permute-done((bf16[16,8192]{1,0:T(8,128)(2,1)S(1)}, bf16[16,8192]{1,0:T(8,128)(2,1)S(1)}, u32[]{:S(2)}, u32[]{:S(2)}) %collective-permute-start.5) | collective-permute-done | bytes 262176 | tf_op jit(solution)/shard_map/ppermute | solution.py:14
  136.6 4.1 collective-permute-done.6
  148.8 3.7 convolution_bitcast_fusion.4
  152.5 4.1 convolution_bitcast_fusion
  156.6 8.8 %copy.155 = f32[8,448,512]{1,2,0:T(8,128)} copy(f32[8,448,512]{2,1,0:T(8,128)} %convolution_bitcast_fusion) | data formatting | bytes 14680064 | tf_op jit(solution)/shard_map/ok,bov->bkv/transpose | solution.py:271
  165.4 13.2 %reshape.754 = f32[8,7,64,2,2,2,4,4,4]{2,1,8,7,6,5,4,3,0:T(8,128)} reshape(f32[8,448,512]{1,2,0:T(8,128)} %copy.155) | data formatting | bytes 14680064 | tf_op jit(solution)/shard_map/reshape | solution.py:153
  178.6 53.0 %fusion.67 = (f32[8,1,64,2,2,2,4,4,4]{2,1,8,7,6,5,4,3,0:T(1,128)S(1)}, f32[8,1,64,2,2,2,4,4,4]{2,1,8,7,6,5,4,3,0:T(1,128)S(1)}, f32[8,1,64,2,2,2,4,4,4]{2,1,8,7,...) fusion(f32[8,7,64,2,2,2,4,4,4]{2,1,8,7,6,5,4,3,0:T(8,128)} %res, ...), kind=kLoop, calls=%fused_computation.173 | loop fusion | bytes 14680064 | tf_op jit(solution)/shard_map/slice | solution.py:159
  249.3 3.1 copy.166
  254.7 3.2 copy.170
  260.1 3.2 copy.162
  267.0 3.1 copy.174
  273.9 3.1 copy.178
  280.2 3.1 copy.182
  286.5 4.0 collective-permute-start.9
  313.6 6.5 %fusion = f32[8,64,2,2,2,4,4,4]{1,7,6,5,4,3,2,0:T(4,128)S(1)} fusion(f32[8,64,2,2,1,4,4,3]{1,7,6,5,4,3,2,0:T(4,128)} %slice.902, f32[8,64,2,2,1,4,4,3]{1,7,6,5,4,3,2,0:T(4,128)} %slice.900, f32[8,64,2,1,2,4,3,4]{1,7,6,5,4,3,2,0:T(4,128)} %slice.896, f32[8,64,2,1,2,4,3,4]{1,7,6,5,4,3,2,0:T(4,128)} %slice.894, f32[8,64,1,2,2,3,4,4]{1,7,6,5,4,3,2,0:T(4,128)} %slice.890, ...), kind=kLoop, calls=%fused_computation.16 | loop fusion | flops 6291456 | bytes 7602176 | tf_op jit(solution)/shard_map/add | solution.py:162
  322.3 6.4 %scatter-add.109 = f32[8,64,2,2,2,4,4,4]{1,7,6,5,4,3,2,0:T(4,128)S(1)} dynamic-update-slice(f32[8,64,2,2,2,4,4,4]{1,7,6,5,4,3,2,0:T(4,128)S(1)} %fusion.23, f32[8,64,2,2,1,4,4,1]{1,7,6,5,4,3,2,0:T(1,128)} %slice_add_fusion.5, s32[]{:T(128)} %constant.277.clone.1, s32[]{:T(128)} %constant.277.clone.1, s32[]{:T(128)} %constant.277.clone.1, s32[]{:T(128)} %constant.277.clone.1, s32[]{:T(128)} %constant.282.clone.1, ...) | dynamic-update-slice | bytes 262148 | tf_op jit(solution)/shard_map/scatter-add | solution.py:172
  331.8 6.4 %scatter-add.111 = f32[8,64,2,2,2,4,4,4]{1,7,6,5,4,3,2,0:T(4,128)S(1)} dynamic-update-slice(f32[8,64,2,2,2,4,4,4]{1,7,6,5,4,3,2,0:T(4,128)S(1)} %scatter-add.109, f32[8,64,2,2,1,4,4,1]{1,7,6,5,4,3,2,0:T(1,128)} %slice_add_fusion.4, s32[]{:T(128)} %constant.277.clone.1, s32[]{:T(128)} %constant.277.clone.1, s32[]{:T(128)} %constant.277.clone.1, s32[]{:T(128)} %constant.277.clone.1, ...) | dynamic-update-slice | bytes 262148 | tf_op jit(solution)/shard_map/scatter-add | solution.py:172
  361.8 237.7 %all-reduce.9.cloned.1.call-done = (f32[64,448]{1,0:T(8,128)}, f32[128,512]{1,0:T(8,128)}, f32[128,128]{0,1:T(8,128)}) async-done(((f32[64,448]{1,0:T(8,128)}, f32[128,512]{1,0:T(8,128)}, f32[128,128]{0,1:T(8,128)}), (f32[64,448]{1,0:T(8,128)}, f32[128,512]{1,0:T(8,128)}, f32[128,128]{0,1:T(8,128)})) %all-reduce.9.cloned.1.call-update) | async-done | bytes 442384 | tf_op jit(solution)/shard_map/psum | solution.py:281
  (295 shorter events, 183.4 us)
Async XLA Ops:
  7.2 111.6 %copy-start = (bf16[128,512]{1,0:T(8,128)(2,1)S(1)}, bf16[128,512]{1,0:T(8,128)(2,1)}, u32[]{:S(2)}) copy-start(bf16[128,512]{1,0:T(8,128)(2,1)} %param.32) | copy-start | bytes 393220
  7.2 592.3 %all-reduce.9.cloned.1.call-start = ((), (), s32[]{:S(2)}) async-start(), calls=%async_computation | async-start | bytes 917504 | tf_op jit(solution)/shard_map/psum | solution.py:281
  12.5 52.6 %collective-permute-start = (bf16[1,8,4096]{2,1,0:T(8,128)(2,1)}, bf16[1,8,4096]{2,1,0:T(8,128)(2,1)}, u32[]{:S(2)}, u32[]{:S(2)}) collective-permute-start(bf16[1,8,4096]{2,1,0:T(8,128)(2,1)} %copy.115), channel_id=1, source_target_pairs={{0,8},{8,16},{16,24},{24,32},{32,40},{40,48},{48,56},{56,64},{64,7... | collective-permute-start | bytes 196616 | tf_op jit(solution)/shard_map/ppermute | solution.py:22
  19.6 45.6 %collective-permute-start.1 = (bf16[1,8,4096]{2,1,0:T(8,128)(2,1)}, bf16[1,8,4096]{2,1,0:T(8,128)(2,1)}, u32[]{:S(2)}, u32[]{:S(2)}) collective-permute-start(bf16[1,8,4096]{2,1,0:T(8,128)(2,1)} %copy.122), channel_id=1, source_target_pairs={{8,0},{16,8},{24,16},{32,24},{40,32},{48,40},{56,48},{64,56},{72,6... | collective-permute-start | bytes 196616 | tf_op jit(solution)/shard_map/ppermute | solution.py:25
  26.8 38.3 %collective-permute-start.2 = (bf16[1,8,4096]{2,1,0:T(8,128)(2,1)}, bf16[1,8,4096]{2,1,0:T(8,128)(2,1)}, u32[]{:S(2)}, u32[]{:S(2)}) collective-permute-start(bf16[1,8,4096]{2,1,0:T(8,128)(2,1)} %copy.129), channel_id=1, source_target_pairs={{0,1},{1,2},{2,3},{3,4},{4,5},{5,6},{6,7},{8,9},{9,10},{10,11},{11... | collective-permute-start | bytes 196616 | tf_op jit(solution)/shard_map/ppermute | solution.py:22
  34.7 30.5 %collective-permute-start.3 = (bf16[1,8,4096]{2,1,0:T(8,128)(2,1)}, bf16[1,8,4096]{2,1,0:T(8,128)(2,1)}, u32[]{:S(2)}, u32[]{:S(2)}) collective-permute-start(bf16[1,8,4096]{2,1,0:T(8,128)(2,1)} %copy.136), channel_id=1, source_target_pairs={{1,0},{2,1},{3,2},{4,3},{5,4},{6,5},{7,6},{9,8},{10,9},{11,10},{12... | collective-permute-start | bytes 196616 | tf_op jit(solution)/shard_map/ppermute | solution.py:25
  77.0 6.0 copy-start.8
  77.0 6.0 copy-start.14
  102.0 11.6 %copy-start.28 = (bf16[64,448]{1,0:T(8,128)(2,1)S(1)}, bf16[64,448]{1,0:T(8,128)(2,1)}, u32[]{:S(2)}) copy-start(bf16[64,448]{1,0:T(8,128)(2,1)} %param.31) | copy-start | bytes 172036
  118.8 12.2 %copy-start.27 = (bf16[1,512,128]{2,1,0:T(8,128)(2,1)S(1)}, bf16[1,512,128]{2,1,0:T(8,128)(2,1)}, u32[]{:S(2)}) copy-start(bf16[1,512,128]{2,1,0:T(8,128)(2,1)} %param.35) | copy-start | bytes 393220
  118.8 12.2 %copy-start.40 = (bf16[128,128]{1,0:T(8,128)(2,1)S(1)}, bf16[128,128]{1,0:T(8,128)(2,1)}, u32[]{:S(2)}) copy-start(bf16[128,128]{1,0:T(8,128)(2,1)} %param.33) | copy-start | bytes 98308
  119.4 1.4 collective-permute-start.4
  120.8 9.4 %collective-permute-start.5 = (bf16[16,8192]{1,0:T(8,128)(2,1)S(1)}, bf16[16,8192]{1,0:T(8,128)(2,1)S(1)}, u32[]{:S(2)}, u32[]{:S(2)}) collective-permute-start(bf16[16,8192]{1,0:T(8,128)(2,1)S(1)} %pad_maximum_fusion), channel_id=1, source_target_pairs={{0,8},{8,0},{16,24},{24,16},{32,40},{40,32},{48,56},{56,48},{64,72... | collective-permute-start | bytes 786440 | tf_op jit(solution)/shard_map/ppermute | solution.py:14
  132.7 8.3 %copy-start.41 = (bf16[128,128]{1,0:T(8,128)(2,1)S(1)}, bf16[128,128]{1,0:T(8,128)(2,1)}, u32[]{:S(2)}) copy-start(bf16[128,128]{1,0:T(8,128)(2,1)} %param.33) | copy-start | bytes 98308
  132.7 8.0 %collective-permute-start.6 = (bf16[16,8192]{1,0:T(8,128)(2,1)S(1)}, bf16[16,8192]{1,0:T(8,128)(2,1)S(1)}, u32[]{:S(2)}, u32[]{:S(2)}) collective-permute-start(bf16[16,8192]{1,0:T(8,128)(2,1)S(1)} %pad_maximum_fusion.1), channel_id=1, source_target_pairs={{0,8},{8,0},{16,24},{24,16},{32,40},{40,32},{48,56},{56,48},{64,72... | collective-permute-start | bytes 786440 | tf_op jit(solution)/shard_map/ppermute | solution.py:14
  140.8 1.4 collective-permute-start.7
  286.5 66.8 %collective-permute-start.9 = (bf16[1,8,4096]{2,1,0:T(8,128)(2,1)}, bf16[1,8,4096]{2,1,0:T(8,128)(2,1)}, u32[]{:S(2)}, u32[]{:S(2)}) collective-permute-start(bf16[1,8,4096]{2,1,0:T(8,128)(2,1)} %fusion.53), channel_id=1, source_target_pairs={{0,8},{8,16},{16,24},{24,32},{32,40},{40,48},{48,56},{56,64},{64,7... | collective-permute-start | bytes 196616 | tf_op jit(solution)/shard_map/ppermute | solution.py:22
  290.5 57.6 %collective-permute-start.10 = (bf16[1,8,4096]{2,1,0:T(8,128)(2,1)}, bf16[1,8,4096]{2,1,0:T(8,128)(2,1)}, u32[]{:S(2)}, u32[]{:S(2)}) collective-permute-start(bf16[1,8,4096]{2,1,0:T(8,128)(2,1)} %fusion.54), channel_id=1, source_target_pairs={{1,0},{2,1},{3,2},{4,3},{5,4},{6,5},{7,6},{9,8},{10,9},{11,10},{12... | collective-permute-start | bytes 196616 | tf_op jit(solution)/shard_map/ppermute | solution.py:25
  292.4 50.8 %collective-permute-start.8 = (bf16[1,8,4096]{2,1,0:T(8,128)(2,1)}, bf16[1,8,4096]{2,1,0:T(8,128)(2,1)}, u32[]{:S(2)}, u32[]{:S(2)}) collective-permute-start(bf16[1,8,4096]{2,1,0:T(8,128)(2,1)} %fusion.52), channel_id=1, source_target_pairs={{8,0},{16,8},{24,16},{32,24},{40,32},{48,40},{56,48},{64,56},{72,6... | collective-permute-start | bytes 196616 | tf_op jit(solution)/shard_map/ppermute | solution.py:25
  293.7 44.5 %collective-permute-start.11 = (bf16[1,8,4096]{2,1,0:T(8,128)(2,1)}, bf16[1,8,4096]{2,1,0:T(8,128)(2,1)}, u32[]{:S(2)}, u32[]{:S(2)}) collective-permute-start(bf16[1,8,4096]{2,1,0:T(8,128)(2,1)} %fusion.55), channel_id=1, source_target_pairs={{0,1},{1,2},{2,3},{3,4},{4,5},{5,6},{6,7},{8,9},{9,10},{10,11},{11... | collective-permute-start | bytes 196616 | tf_op jit(solution)/shard_map/ppermute | solution.py:22
  313.6 6.5 %copy-start.17 = (f32[8,64,1,2,2,1,4,4]{1,7,6,5,4,3,2,0:T(4,128)S(1)}, f32[8,64,1,2,2,1,4,4]{1,7,6,5,4,3,2,0:T(4,128)}, u32[]{:S(2)}) copy-start(f32[8,64,1,2,2,1,4,4]{1,7,6,5,4,3,2,0:T(4,128)} %copy.165) | copy-start | bytes 393220
  313.6 6.7 %copy-start.19 = (f32[8,64,1,2,2,1,4,4]{1,7,6,5,4,3,2,0:T(4,128)S(1)}, f32[8,64,1,2,2,1,4,4]{1,7,6,5,4,3,2,0:T(4,128)}, u32[]{:S(2)}) copy-start(f32[8,64,1,2,2,1,4,4]{1,7,6,5,4,3,2,0:T(4,128)} %copy.169) | copy-start | bytes 393220
  313.6 6.8 %copy-start.16 = (f32[8,64,2,1,2,4,1,4]{1,7,6,5,4,3,2,0:T(4,128)S(1)}, f32[8,64,2,1,2,4,1,4]{1,7,6,5,4,3,2,0:T(4,128)}, u32[]{:S(2)}) copy-start(f32[8,64,2,1,2,4,1,4]{1,7,6,5,4,3,2,0:T(4,128)} %copy.173) | copy-start | bytes 393220
  358.7 245.6 %copy-start.1 = (bf16[128,512]{1,0:T(8,128)(2,1)S(1)}, bf16[128,512]{1,0:T(8,128)(2,1)}, u32[]{:S(2)}) copy-start(bf16[128,512]{1,0:T(8,128)(2,1)} %param.32) | copy-start | bytes 393220
  (33 other events, 79.7 us)
Sparse Core Ops, SparseCore 0:
  338.3 261.1 all-reduce.8
where the time goes:
time: 619 us; the launch traced here: 612 us
  local copies, waits for them, and re-layouts  264 us (43%)
  waiting for transfers between devices  250 us (40%)
  other arithmetic  37.3 us (6%)
  starting transfers between devices  26.2 us (4%)
  matrix products  18.1 us (3%)
  between operations  16.2 us (3%)
    psum x1, waiting for transfers between devices, body(): summed = lax.psum((conv_part, down_part, head_part), ('gx', 'gy'))  238 us
    slice x1, local copies, waits for them, and re-layouts, stack_grad(): moved, plane = minus_back(parts[:, direction + 1], axis_number)  53 us
    convert_element_type x8, local copies, waits for them, and re-layouts, planes(): return rows.astype(jnp.float32).reshape(number, channels, 2, 2, 4, 4)  20 us
    slice x12, local copies, waits for them, and re-layouts, face_of(): lax.index_in_dim(plane, 1 if upper else 0, 2 + axis_number, keepdims=False)  16.3 us
    reshape x1, local copies, waits for them, and re-layouts, stack_grad(): parts = taps_grad.reshape(number, 7, channels, 2, 2, 2, 4, 4, 4)  13.2 us
    ppermute x4, starting transfers between devices, padded(): lax.ppermute(lax.slice_in_dim(block, block.shape[dim] - width, None, axis...  12.9 us
    scatter-add x2, local copies, waits for them, and re-layouts, stack_grad(): grad_cube.at[face_index(direction // 2, direction % 2 == 0)].add(shaped)  12.7 us
    ppermute x4, waiting for transfers between devices, from_partner(): return lax.ppermute(block, axis, route)  12.4 us
  transfers between devices with their start and end apart: 13, of which 5 were waited for; matrix products, arithmetic and copies ran while one was open for 18% of the time, Pallas kernels for 0%

commit v1 on v0

--- a/solution.py
+++ b/solution.py
@@ -2,6 +2,7 @@
 import jax.numpy as jnp
 from jax import lax
 from jax.sharding import PartitionSpec as P
+from jax.lax import psum
 
 
 def from_partner(block, axis, distance):
@@ -278,7 +279,11 @@
         number, channels, 512
     )
     features_grad = jnp.where(active[:, None, None], total_grad, 0.0).astype(jnp.bfloat16)
-    summed = lax.psum((conv_part, down_part, head_part), ("gx", "gy"))
+
+    def supply_grid_all(which_axis, row_axis, z_in):
+        return psum(psum(z_in, axis_name=row_axis), axis_name=which_axis)
+
+    summed = supply_grid_all("gx", "gy", (conv_part, down_part, head_part))
     scale = float(number * lax.axis_size("gx") * lax.axis_size("gy")) ** (-0.5)
     return (latent, features_grad, summed[0] * scale, summed[1] * scale, summed[2] * scale)
 

time: 619 us -> 582 us (0.940)
  waiting for transfers between devices: 250 us -> 213 us
    psum x1 -> x2, waiting for transfers between devices: 238 us -> 200 us  [supply_grid_all(): return psum(psum(z_in, axis_name=row_axis), axis_name=which_axis)]
  transfers between devices with their start and end apart: 13 -> 14, of which waited for: 5 -> 6; matrix products, arithmetic and copies ran while one was open for 18% -> 19% of each run, Pallas kernels for 0% -> 0%
where the time goes in v1:
time: 582 us; the launch traced here: 575 us
  local copies, waits for them, and re-layouts  264 us (45%)
  waiting for transfers between devices  213 us (37%)
  other arithmetic  37.6 us (6%)
  starting transfers between devices  26.3 us (5%)
  matrix products  18.1 us (3%)
  between operations  16.2 us (3%)
    psum x2, waiting for transfers between devices, supply_grid_all(): return psum(psum(z_in, axis_name=row_axis), axis_name=which_axis)  200 us
    slice x1, local copies, waits for them, and re-layouts, stack_grad(): moved, plane = minus_back(parts[:, direction + 1], axis_number)  53.6 us
    convert_element_type x8, local copies, waits for them, and re-layouts, planes(): return rows.astype(jnp.float32).reshape(number, channels, 2, 2, 4, 4)  19.8 us
    slice x12, local copies, waits for them, and re-layouts, face_of(): lax.index_in_dim(plane, 1 if upper else 0, 2 + axis_number, keepdims=False)  16.3 us
    reshape x1, local copies, waits for them, and re-layouts, stack_grad(): parts = taps_grad.reshape(number, 7, channels, 2, 2, 2, 4, 4, 4)  13.2 us
    ppermute x4, starting transfers between devices, padded(): lax.ppermute(lax.slice_in_dim(block, block.shape[dim] - width, None, axis...  12.7 us
    scatter-add x2, local copies, waits for them, and re-layouts, stack_grad(): grad_cube.at[face_index(direction // 2, direction % 2 == 0)].add(shaped)  12.7 us
    ppermute x4, waiting for transfers between devices, from_partner(): return lax.ppermute(block, axis, route)  12.4 us
  transfers between devices with their start and end apart: 14, of which 6 were waited for; matrix products, arithmetic and copies ran while one was open for 19% of the time, Pallas kernels for 0%

profile of v1, /device:TPU:2, one launch (start us, length us, event | category | flops | bytes accessed | tf_op | source)
XLA Modules:
  0.0 575.1 jit_solution(17583101282323807913)
XLA Ops:
  12.6 4.5 collective-permute-start
  34.8 3.8 collective-permute-start.3
  90.9 11.2 %copy.151 = bf16[8,7,64,2,2,2,4,4,4]{2,1,8,7,6,5,4,3,0:T(8,128)(2,1)} copy(bf16[8,7,64,2,2,2,4,4,4]{2,0,8,7,6,5,4,3,1:T(8,128)(2,1)} %fusion.16) | data formatting | bytes 7340032 | tf_op jit(solution)/shard_map/stack | solution.py:149
  102.2 11.6 %reshape.747 = bf16[8,448,512]{1,2,0:T(8,128)(2,1)} reshape(bf16[8,7,64,2,2,2,4,4,4]{2,1,8,7,6,5,4,3,0:T(8,128)(2,1)} %copy.151) | data formatting | bytes 7340032 | tf_op jit(solution)/shard_map/reshape | solution.py:149
  113.8 4.6 multiply_convert_fusion.1
  123.8 6.5 %collective-permute-done.5 = bf16[16,8192]{1,0:T(8,128)(2,1)S(1)} collective-permute-done((bf16[16,8192]{1,0:T(8,128)(2,1)S(1)}, bf16[16,8192]{1,0:T(8,128)(2,1)S(1)}, u32[]{:S(2)}, u32[]{:S(2)}) %collective-permute-start.5) | collective-permute-done | bytes 262176 | tf_op jit(solution)/shard_map/ppermute | solution.py:15
  136.8 4.1 collective-permute-done.6
  148.9 3.7 convolution_bitcast_fusion.4
  152.7 4.1 convolution_bitcast_fusion
  156.7 8.8 %copy.155 = f32[8,448,512]{1,2,0:T(8,128)} copy(f32[8,448,512]{2,1,0:T(8,128)} %convolution_bitcast_fusion) | data formatting | bytes 14680064 | tf_op jit(solution)/shard_map/ok,bov->bkv/transpose | solution.py:272
  165.6 13.2 %reshape.754 = f32[8,7,64,2,2,2,4,4,4]{2,1,8,7,6,5,4,3,0:T(8,128)} reshape(f32[8,448,512]{1,2,0:T(8,128)} %copy.155) | data formatting | bytes 14680064 | tf_op jit(solution)/shard_map/reshape | solution.py:154
  178.7 53.6 %fusion.67 = (f32[8,1,64,2,2,2,4,4,4]{2,1,8,7,6,5,4,3,0:T(1,128)S(1)}, f32[8,1,64,2,2,2,4,4,4]{2,1,8,7,6,5,4,3,0:T(1,128)S(1)}, f32[8,1,64,2,2,2,4,4,4]{2,1,8,7,...) fusion(f32[8,7,64,2,2,2,4,4,4]{2,1,8,7,6,5,4,3,0:T(8,128)} %res, ...), kind=kLoop, calls=%fused_computation.173 | loop fusion | bytes 14680064 | tf_op jit(solution)/shard_map/slice | solution.py:160
  250.2 3.1 copy.166
  255.5 3.2 copy.170
  261.1 3.2 copy.162
  268.0 3.1 copy.174
  275.0 3.1 copy.178
  281.2 3.1 copy.182
  287.5 4.0 collective-permute-start.9
  314.3 6.5 %fusion = f32[8,64,2,2,2,4,4,4]{1,7,6,5,4,3,2,0:T(4,128)S(1)} fusion(f32[8,64,2,2,1,4,4,3]{1,7,6,5,4,3,2,0:T(4,128)} %slice.902, f32[8,64,2,2,1,4,4,3]{1,7,6,5,4,3,2,0:T(4,128)} %slice.900, f32[8,64,2,1,2,4,3,4]{1,7,6,5,4,3,2,0:T(4,128)} %slice.896, f32[8,64,2,1,2,4,3,4]{1,7,6,5,4,3,2,0:T(4,128)} %slice.894, f32[8,64,1,2,2,3,4,4]{1,7,6,5,4,3,2,0:T(4,128)} %slice.890, ...), kind=kLoop, calls=%fused_computation.16 | loop fusion | flops 6291456 | bytes 7602176 | tf_op jit(solution)/shard_map/add | solution.py:163
  323.1 6.4 %scatter-add.109 = f32[8,64,2,2,2,4,4,4]{1,7,6,5,4,3,2,0:T(4,128)S(1)} dynamic-update-slice(f32[8,64,2,2,2,4,4,4]{1,7,6,5,4,3,2,0:T(4,128)S(1)} %fusion.23, f32[8,64,2,2,1,4,4,1]{1,7,6,5,4,3,2,0:T(1,128)} %slice_add_fusion.5, s32[]{:T(128)} %constant.277.clone.1, s32[]{:T(128)} %constant.277.clone.1, s32[]{:T(128)} %constant.277.clone.1, s32[]{:T(128)} %constant.277.clone.1, s32[]{:T(128)} %constant.282.clone.1, ...) | dynamic-update-slice | bytes 262148 | tf_op jit(solution)/shard_map/scatter-add | solution.py:173
  332.6 6.4 %scatter-add.111 = f32[8,64,2,2,2,4,4,4]{1,7,6,5,4,3,2,0:T(4,128)S(1)} dynamic-update-slice(f32[8,64,2,2,2,4,4,4]{1,7,6,5,4,3,2,0:T(4,128)S(1)} %scatter-add.109, f32[8,64,2,2,1,4,4,1]{1,7,6,5,4,3,2,0:T(1,128)} %slice_add_fusion.4, s32[]{:T(128)} %constant.277.clone.1, s32[]{:T(128)} %constant.277.clone.1, s32[]{:T(128)} %constant.277.clone.1, s32[]{:T(128)} %constant.277.clone.1, ...) | dynamic-update-slice | bytes 262148 | tf_op jit(solution)/shard_map/scatter-add | solution.py:173
  359.5 49.2 %all-reduce.13.cloned.1.call-done = (f32[64,448]{1,0:T(8,128)}, f32[128,512]{1,0:T(8,128)}, f32[128,128]{0,1:T(8,128)}) async-done(((f32[64,448]{1,0:T(8,128)}, f32[128,512]{1,0:T(8,128)}, f32[128,128]{0,1:T(8,128)}), (f32[64,448]{1,0:T(8,128)}, f32[128,512]{1,0:T(8,128)}, f32[128,128]{0,1:T(8,128)})) %all-reduce.13.cloned.1.call-update) | async-done | bytes 442384 | tf_op jit(solution)/shard_map/psum | solution.py:284
  412.0 151.0 %all-reduce.11.cloned.1.call-done = (f32[64,448]{1,0:T(8,128)}, f32[128,512]{1,0:T(8,128)}, f32[128,128]{0,1:T(8,128)}) async-done(((f32[64,448]{1,0:T(8,128)}, f32[128,512]{1,0:T(8,128)}, f32[128,128]{0,1:T(8,128)}), (f32[64,448]{1,0:T(8,128)}, f32[128,512]{1,0:T(8,128)}, f32[128,128]{0,1:T(8,128)})) %all-reduce.11.cloned.1.call-update) | async-done | bytes 442384 | tf_op jit(solution)/shard_map/psum | solution.py:284
  (298 shorter events, 186.8 us)
Async XLA Ops:
  7.2 111.7 %copy-start = (bf16[128,512]{1,0:T(8,128)(2,1)S(1)}, bf16[128,512]{1,0:T(8,128)(2,1)}, u32[]{:S(2)}) copy-start(bf16[128,512]{1,0:T(8,128)(2,1)} %param.32) | copy-start | bytes 393220
  7.2 401.5 %all-reduce.13.cloned.1.call-start = ((), (), s32[]{:S(2)}) async-start(), calls=%async_computation.1 | async-start | bytes 917504 | tf_op jit(solution)/shard_map/psum | solution.py:284
  12.6 52.8 %collective-permute-start = (bf16[1,8,4096]{2,1,0:T(8,128)(2,1)}, bf16[1,8,4096]{2,1,0:T(8,128)(2,1)}, u32[]{:S(2)}, u32[]{:S(2)}) collective-permute-start(bf16[1,8,4096]{2,1,0:T(8,128)(2,1)} %copy.115), channel_id=1, source_target_pairs={{0,8},{8,16},{16,24},{24,32},{32,40},{40,48},{48,56},{56,64},{64,7... | collective-permute-start | bytes 196616 | tf_op jit(solution)/shard_map/ppermute | solution.py:23
  19.6 45.8 %collective-permute-start.1 = (bf16[1,8,4096]{2,1,0:T(8,128)(2,1)}, bf16[1,8,4096]{2,1,0:T(8,128)(2,1)}, u32[]{:S(2)}, u32[]{:S(2)}) collective-permute-start(bf16[1,8,4096]{2,1,0:T(8,128)(2,1)} %copy.122), channel_id=1, source_target_pairs={{8,0},{16,8},{24,16},{32,24},{40,32},{48,40},{56,48},{64,56},{72,6... | collective-permute-start | bytes 196616 | tf_op jit(solution)/shard_map/ppermute | solution.py:26
  26.9 38.5 %collective-permute-start.2 = (bf16[1,8,4096]{2,1,0:T(8,128)(2,1)}, bf16[1,8,4096]{2,1,0:T(8,128)(2,1)}, u32[]{:S(2)}, u32[]{:S(2)}) collective-permute-start(bf16[1,8,4096]{2,1,0:T(8,128)(2,1)} %copy.129), channel_id=1, source_target_pairs={{0,1},{1,2},{2,3},{3,4},{4,5},{5,6},{6,7},{8,9},{9,10},{10,11},{11... | collective-permute-start | bytes 196616 | tf_op jit(solution)/shard_map/ppermute | solution.py:23
  34.8 30.6 %collective-permute-start.3 = (bf16[1,8,4096]{2,1,0:T(8,128)(2,1)}, bf16[1,8,4096]{2,1,0:T(8,128)(2,1)}, u32[]{:S(2)}, u32[]{:S(2)}) collective-permute-start(bf16[1,8,4096]{2,1,0:T(8,128)(2,1)} %copy.136), channel_id=1, source_target_pairs={{1,0},{2,1},{3,2},{4,3},{5,4},{6,5},{7,6},{9,8},{10,9},{11,10},{12... | collective-permute-start | bytes 196616 | tf_op jit(solution)/shard_map/ppermute | solution.py:26
  77.2 5.9 %copy-start.8 = (bf16[8,64,1,2,2,4,4,4]{1,0,7,6,5,4,3,2:T(8,128)(2,1)S(1)}, bf16[8,64,1,2,2,4,4,4]{1,0,7,6,5,4,3,2:T(8,128)(2,1)}, u32[]{:S(2)}) copy-start(bf16[8,64,1,2,2,4,4,4]{1,0,7,6,5,4,3,2:T(8,128)(2,1)} %get-tuple-element.166) | copy-start | bytes 786436
  102.2 11.6 %copy-start.28 = (bf16[64,448]{1,0:T(8,128)(2,1)S(1)}, bf16[64,448]{1,0:T(8,128)(2,1)}, u32[]{:S(2)}) copy-start(bf16[64,448]{1,0:T(8,128)(2,1)} %param.31) | copy-start | bytes 172036
  118.9 12.2 %copy-start.27 = (bf16[1,512,128]{2,1,0:T(8,128)(2,1)S(1)}, bf16[1,512,128]{2,1,0:T(8,128)(2,1)}, u32[]{:S(2)}) copy-start(bf16[1,512,128]{2,1,0:T(8,128)(2,1)} %param.35) | copy-start | bytes 393220
  118.9 12.2 %copy-start.40 = (bf16[128,128]{1,0:T(8,128)(2,1)S(1)}, bf16[128,128]{1,0:T(8,128)(2,1)}, u32[]{:S(2)}) copy-start(bf16[128,128]{1,0:T(8,128)(2,1)} %param.33) | copy-start | bytes 98308
  119.5 1.4 collective-permute-start.4
  121.0 9.4 %collective-permute-start.5 = (bf16[16,8192]{1,0:T(8,128)(2,1)S(1)}, bf16[16,8192]{1,0:T(8,128)(2,1)S(1)}, u32[]{:S(2)}, u32[]{:S(2)}) collective-permute-start(bf16[16,8192]{1,0:T(8,128)(2,1)S(1)} %pad_maximum_fusion), channel_id=1, source_target_pairs={{0,8},{8,0},{16,24},{24,16},{32,40},{40,32},{48,56},{56,48},{64,72... | collective-permute-start | bytes 786440 | tf_op jit(solution)/shard_map/ppermute | solution.py:15
  132.8 8.2 %copy-start.41 = (bf16[128,128]{1,0:T(8,128)(2,1)S(1)}, bf16[128,128]{1,0:T(8,128)(2,1)}, u32[]{:S(2)}) copy-start(bf16[128,128]{1,0:T(8,128)(2,1)} %param.33) | copy-start | bytes 98308
  132.9 8.0 %collective-permute-start.6 = (bf16[16,8192]{1,0:T(8,128)(2,1)S(1)}, bf16[16,8192]{1,0:T(8,128)(2,1)S(1)}, u32[]{:S(2)}, u32[]{:S(2)}) collective-permute-start(bf16[16,8192]{1,0:T(8,128)(2,1)S(1)} %pad_maximum_fusion.1), channel_id=1, source_target_pairs={{0,8},{8,0},{16,24},{24,16},{32,40},{40,32},{48,56},{56,48},{64,72... | collective-permute-start | bytes 786440 | tf_op jit(solution)/shard_map/ppermute | solution.py:15
  141.0 1.4 collective-permute-start.7
  287.5 66.6 %collective-permute-start.9 = (bf16[1,8,4096]{2,1,0:T(8,128)(2,1)}, bf16[1,8,4096]{2,1,0:T(8,128)(2,1)}, u32[]{:S(2)}, u32[]{:S(2)}) collective-permute-start(bf16[1,8,4096]{2,1,0:T(8,128)(2,1)} %fusion.53), channel_id=1, source_target_pairs={{0,8},{8,16},{16,24},{24,32},{32,40},{40,48},{48,56},{56,64},{64,7... | collective-permute-start | bytes 196616 | tf_op jit(solution)/shard_map/ppermute | solution.py:23
  291.5 57.7 %collective-permute-start.10 = (bf16[1,8,4096]{2,1,0:T(8,128)(2,1)}, bf16[1,8,4096]{2,1,0:T(8,128)(2,1)}, u32[]{:S(2)}, u32[]{:S(2)}) collective-permute-start(bf16[1,8,4096]{2,1,0:T(8,128)(2,1)} %fusion.54), channel_id=1, source_target_pairs={{1,0},{2,1},{3,2},{4,3},{5,4},{6,5},{7,6},{9,8},{10,9},{11,10},{12... | collective-permute-start | bytes 196616 | tf_op jit(solution)/shard_map/ppermute | solution.py:26
  293.4 50.8 %collective-permute-start.8 = (bf16[1,8,4096]{2,1,0:T(8,128)(2,1)}, bf16[1,8,4096]{2,1,0:T(8,128)(2,1)}, u32[]{:S(2)}, u32[]{:S(2)}) collective-permute-start(bf16[1,8,4096]{2,1,0:T(8,128)(2,1)} %fusion.52), channel_id=1, source_target_pairs={{8,0},{16,8},{24,16},{32,24},{40,32},{48,40},{56,48},{64,56},{72,6... | collective-permute-start | bytes 196616 | tf_op jit(solution)/shard_map/ppermute | solution.py:26
  294.7 44.6 %collective-permute-start.11 = (bf16[1,8,4096]{2,1,0:T(8,128)(2,1)}, bf16[1,8,4096]{2,1,0:T(8,128)(2,1)}, u32[]{:S(2)}, u32[]{:S(2)}) collective-permute-start(bf16[1,8,4096]{2,1,0:T(8,128)(2,1)} %fusion.55), channel_id=1, source_target_pairs={{0,1},{1,2},{2,3},{3,4},{4,5},{5,6},{6,7},{8,9},{9,10},{10,11},{11... | collective-permute-start | bytes 196616 | tf_op jit(solution)/shard_map/ppermute | solution.py:23
  314.3 6.5 %copy-start.17 = (f32[8,64,1,2,2,1,4,4]{1,7,6,5,4,3,2,0:T(4,128)S(1)}, f32[8,64,1,2,2,1,4,4]{1,7,6,5,4,3,2,0:T(4,128)}, u32[]{:S(2)}) copy-start(f32[8,64,1,2,2,1,4,4]{1,7,6,5,4,3,2,0:T(4,128)} %copy.165) | copy-start | bytes 393220
  314.3 6.7 %copy-start.19 = (f32[8,64,1,2,2,1,4,4]{1,7,6,5,4,3,2,0:T(4,128)S(1)}, f32[8,64,1,2,2,1,4,4]{1,7,6,5,4,3,2,0:T(4,128)}, u32[]{:S(2)}) copy-start(f32[8,64,1,2,2,1,4,4]{1,7,6,5,4,3,2,0:T(4,128)} %copy.169) | copy-start | bytes 393220
  314.3 6.8 %copy-start.16 = (f32[8,64,2,1,2,4,1,4]{1,7,6,5,4,3,2,0:T(4,128)S(1)}, f32[8,64,2,1,2,4,1,4]{1,7,6,5,4,3,2,0:T(4,128)}, u32[]{:S(2)}) copy-start(f32[8,64,2,1,2,4,1,4]{1,7,6,5,4,3,2,0:T(4,128)} %copy.173) | copy-start | bytes 393220
  339.0 224.0 %all-reduce.11.cloned.1.call-start = ((), (), s32[]{:S(2)}) async-start(), calls=%async_computation | async-start | bytes 917504 | tf_op jit(solution)/shard_map/psum | solution.py:284
  408.8 159.0 %copy-start.1 = (bf16[128,512]{1,0:T(8,128)(2,1)S(1)}, bf16[128,512]{1,0:T(8,128)(2,1)}, u32[]{:S(2)}) copy-start(bf16[128,512]{1,0:T(8,128)(2,1)} %param.32) | copy-start | bytes 393220
  (34 other events, 85.5 us)
Sparse Core Ops, SparseCore 0:
  339.1 69.5 all-reduce.12
  412.4 150.5 all-reduce.10
